TPU v7x, 32 devices: a whole 2x2x4 slice. The times are simulated.
32 devices in a mesh: parts: 2 (over y), rows: 4 (over z), ex: 4 (over x, core).
Axes of the slice: x: 2, y: 2, z: 4, core: 2. Of those that a mesh axis runs over, the one named last changes fastest.
Arguments:
- hidden_acts: bfloat16 [1024, 512], P(('parts', 'ex'), 'rows'), parts along dimension 0, may hold values from -6 to 6
- cotangent: bfloat16 [1024, 4096], P(('parts', 'ex'), 'rows'), parts along dimension 0, may hold values from -0.796875 to 0.796875
- lengths: int32 [64], P('parts'), parts along dimension 0, may hold values from 1 to 64, 512 in all
- row_signs: int32 [512], P('rows'), may hold values from -1 to 1, as said below
- col_signs: int32 [4096], replicated, may hold values from -1 to 1, as said below
- feat_row: int32 [8192], replicated, may hold values from 0 to 511
- feat_col: int32 [8192], replicated, may hold values from 0 to 4095
- inverse_rows: bfloat16 [8192, 8192], P('rows'), as said below
Outputs:
- scores: bfloat16 [64, 8192], P(('parts', 'ex'), 'rows'), parts along dimension 0
There are 2 independent parts, one for each index of `parts`. A program takes and returns all parts, laid end to end along the dimension named above; an argument that names none is the same for every part. Nothing has to cross between parts.
Inputs may be any that keep to these rules, and one draw needn't show every extreme that they name: `row_signs`: every entry is -1 or +1. `col_signs`: every entry is -1 or +1. `inverse_rows`: the whole matrix equals its transpose. The lengths sum to 512 and the largest equals 64.
All inputs are finite; a program needn't handle non-finite values.
Results may differ from a plain program's by a relative error of at most 0.0049.
Values may be sent and summed in bfloat16 or wider, within the bound.
A program may use at most 128 MiB of HBM per device.

v0:
```python
import math

import jax
import jax.numpy as jnp
from jax import lax
from jax.sharding import PartitionSpec as P

exact_mode = lax.Precision.HIGHEST


def hadamard(mat_size):
    indices = jnp.arange(mat_size, dtype=jnp.int32)
    common = indices[:, None] & indices[None, :]
    parity = jnp.zeros((mat_size, mat_size), jnp.int32)
    for bit_pos in range(max(mat_size.bit_length() - 1, 0)):
        parity = parity + (common >> bit_pos & 1)
    return (1 - 2 * (parity % 2)).astype(jnp.float32)


def sign_of(first_bits, second_bits, bit_count):
    parity = jnp.zeros_like(first_bits)
    for bit_pos in range(bit_count):
        parity = parity + (first_bits >> bit_pos & second_bits >> bit_pos & 1)
    return (1 - 2 * (parity % 2)).astype(jnp.float32)


def kron_signed(signed, outer_size, inner_size):
    tokens = signed.shape[0]
    shaped = signed.reshape(tokens, outer_size, inner_size)
    shaped = jnp.einsum(
        "tri,ia->tra",
        shaped,
        hadamard(inner_size).astype(jnp.bfloat16),
        preferred_element_type=jnp.float32,
    )
    shaped = jnp.einsum("tra,rh->tha", shaped, hadamard(outer_size), precision=exact_mode)
    return shaped.reshape(tokens, outer_size * inner_size)


def local(hidden_acts, cotangent, lengths, row_signs, col_signs, feat_row, feat_col, inverse_rows):
    row_count = lax.axis_size("rows")
    row_rank = lax.axis_index("rows")
    ex_group = lax.axis_index("ex")
    tok_dev = hidden_acts.shape[0]
    width_dev = hidden_acts.shape[1]
    model_width = col_signs.shape[0]
    feature_count = feat_row.shape[0]
    example_count = lengths.shape[0]
    row_bits = row_count.bit_length() - 1
    norm_scale = 1.0 / math.sqrt(width_dev * row_count * model_width)
    block_rows = min(tok_dev, 128)
    inner_width = min(model_width, 128)
    end_pos = jnp.cumsum(lengths)
    base_pos = ex_group * tok_dev
    example_ids = jnp.arange(example_count, dtype=jnp.int32)
    full_cot = lax.all_gather(cotangent, "rows", axis=1, tiled=True)
    sign_table = hadamard(width_dev) * row_signs.astype(jnp.float32)[:, None]
    left_side = jnp.dot(
        hidden_acts, sign_table.astype(jnp.bfloat16), preferred_element_type=jnp.float32
    )
    signed = full_cot * col_signs.astype(jnp.bfloat16)[None, :]
    right_side = kron_signed(signed, model_width // inner_width, inner_width)
    left_index = feat_row % width_dev
    feature_weight = sign_of(feat_row // width_dev, row_rank, row_bits) * norm_scale

    def one_block(block_id, total):
        products = jnp.take(left_side, left_index, axis=1) * jnp.take(right_side, feat_col, axis=1)
        positions = base_pos + block_id * block_rows + jnp.arange(block_rows, dtype=jnp.int32)
        owner = jnp.sum((positions[:, None] >= end_pos[None, :]).astype(jnp.int32), axis=1)
        member = (example_ids[:, None] == owner[None, :]).astype(jnp.float32)
        return total + jnp.dot(member, products, precision=exact_mode)

    summed = lax.fori_loop(
        0, tok_dev // block_rows, one_block, jnp.zeros((example_count, feature_count), jnp.float32)
    )
    phi_part = summed * feature_weight[None, :]
    by_feature = lax.psum_scatter(phi_part, "rows", scatter_dimension=1, tiled=True)
    phi_own = lax.psum_scatter(by_feature, "ex", scatter_dimension=0, tiled=True)
    phi_low = phi_own.astype(jnp.bfloat16)
    phi_all = lax.all_gather(phi_low, "rows", axis=1, tiled=True)
    scores = lax.dot_general(
        phi_all, inverse_rows, (((1,), (1,)), ((), ())), preferred_element_type=jnp.float32
    )
    return scores.astype(jnp.bfloat16)


def solution(mesh):
    placed = (
        P(("parts", "ex"), "rows"),
        P(("parts", "ex"), "rows"),
        P("parts"),
        P("rows"),
        P(),
        P(),
        P(),
        P("rows", None),
    )
    return jax.shard_map(
        local, mesh=mesh, in_specs=placed, out_specs=P(("parts", "ex"), "rows"), check_vma=False
    )
```

profile of v0, /device:TPU:0, one launch (start us, length us, event | category | flops | bytes accessed | tf_op | source)
XLA Modules:
  0.0 168.0 jit_solution(14677767108908052451)
XLA Ops:
  6.5 0.7 all-gather.2.cloned.1.call-update
  7.3 0.7 convert_element_type.38
  8.0 0.7 convert_element_type.41
  8.7 0.7 copy.13
  9.4 0.1 reduce-window.8
  9.5 0.1 reduce
  9.6 0.8 broadcast_clamp_fusion
  10.4 0.3 convolution_bitcast_fusion.1
  10.7 27.7 %gather_fusion = f32[8192,128]{1,0:T(8,128)} fusion(f32[128,128]{0,1:T(8,128)S(1)} %convolution_bitcast_fusion.1, s32[8192]{0:T(1024)S(1)} %broadcast_clamp_fusion), kind=kCustom, calls=%fused_computation | custom fusion | bytes 8421376 | tf_op jit(solution)/shard_map/while/body/eval_jaxpr/jit(_take)/gather | solution.py:67
  38.4 0.1 convert_reduce_fusion
  38.5 0.1 fusion.14
  38.6 1.0 all-gather.2.cloned.1.call-done
  39.6 1.3 multiply_bitcast_fusion
  40.9 0.2 copy.16
  41.2 0.5 fusion.15
  41.7 3.2 %convolution_bitcast_fusion = f32[128,32,128]{2,1,0:T(8,128)} fusion(f32[128,32,128]{2,1,0:T(8,128)S(1)} %fusion.15), kind=kOutput, calls=%fused_computation.10 | convolution fusion | flops 201356288 | bytes 4194304 | tf_op jit(solution)/shard_map/tra,rh->tha/dot_general | solution.py:36
  44.9 2.0 %copy.15 = f32[128,32,128]{0,2,1:T(8,128)S(1)} copy(f32[128,32,128]{2,1,0:T(8,128)} %convolution_bitcast_fusion) | data formatting | bytes 4194304 | tf_op jit(solution)/shard_map/reshape | solution.py:37
  46.9 27.7 %gather_fusion.1 = f32[8192,128]{1,0:T(8,128)} fusion(f32[128,4096]{0,1:T(8,128)S(1)} %bitcast.20, s32[8192]{0:T(1024)S(1)} %fusion.22), kind=kCustom, calls=%fused_computation.1 | custom fusion | bytes 8421376 | tf_op jit(solution)/shard_map/while/body/eval_jaxpr/jit(_take)/gather | solution.py:67
  74.7 7.2 %convolution_multiply_fusion = f32[32,8192]{1,0:T(8,128)} fusion(f32[8192,128]{1,0:T(8,128)} %gather_fusion.1, f32[8192,128]{1,0:T(8,128)} %gather_fusion, pred[8192]{0:T(1024)(128)(4,1)S(1)} %get-tuple-element.23, pred[8192]{0:T(1024)(128)(4,1)S(1)} %get-tuple-element.24, f32[8192]{0:T(1024)S(1)} %fusion.14, s32[128]{0:T(128)S(1)} %convert_reduce_fusion), kind=kOutput, calls=%fused_computation.2 | convolution fusion | flops 406065152 | bytes 9486848 | tf_op jit(solution)/shard_map/while/body/eval_jaxpr/dot_general | solution.py:71
  82.0 29.1 %reduce-scatter.3.cloned.1.call-done = f32[32,2048]{1,0:T(8,128)} async-done(((f32[32,8192]{1,0:T(8,128)}), f32[32,2048]{1,0:T(8,128)}) %reduce-scatter.3.cloned.1.call-update) | async-done | bytes 262160 | tf_op jit(solution)/shard_map/reduce_scatter | solution.py:77
  111.1 21.1 %reduce-scatter.5.cloned.1.call-done = f32[8,2048]{1,0:T(8,128)} async-done(((f32[32,2048]{1,0:T(8,128)}), f32[8,2048]{1,0:T(8,128)}) %reduce-scatter.5.cloned.1.call-update) | async-done | bytes 65552 | tf_op jit(solution)/shard_map/reduce_scatter | solution.py:78
  132.1 0.8 convert_element_type.44
  133.0 13.4 %all_gather.7 = bf16[8,8192]{1,0:T(8,128)(2,1)S(1)} all-gather(bf16[8,2048]{1,0:T(8,128)(2,1)S(1)} %convert_element_type.44), channel_id=1, replica_groups=mesh['parts'=2,'rows'=4,'ex'=4] {'rows'}, dimensions={1}, use_global_device_ids=true | all-gather | bytes 163840 | tf_op jit(solution)/shard_map/all_gather | solution.py:80
  146.4 15.1 %convolution_convert_fusion = bf16[8,2048]{1,0:T(8,128)(2,1)} fusion(bf16[8,8192]{1,0:T(8,128)(2,1)S(1)} %all_gather.7, bf16[2048,8192]{1,0:T(8,128)(2,1)} %param.15), kind=kOutput, calls=%fused_computation.6 | convolution fusion | flops 268451840 | bytes 33718272 | tf_op jit(solution)/shard_map/dot_general | solution.py:81
  (14 shorter events, 0.2 us)
Async XLA Ops:
  6.5 3.9 %copy-start = (bf16[128,128]{1,0:T(8,128)(2,1)S(1)}, bf16[128,128]{1,0:T(8,128)(2,1)}, u32[]{:S(2)}) copy-start(bf16[128,128]{1,0:T(8,128)(2,1)} %param.8) | copy-start | bytes 98308
  6.5 33.1 %all-gather.2.cloned.1.call-start = ((), (), s32[]{:S(2)}) async-start(), calls=%async_computation.2 | async-start | bytes 1310720 | tf_op jit(solution)/shard_map/all_gather | solution.py:56
  7.3 103.8 %reduce-scatter.3.cloned.1.call-start = ((), (), s32[]{:S(2)}) async-start(), calls=%async_computation.3 | async-start | bytes 1310720 | tf_op jit(solution)/shard_map/reduce_scatter | solution.py:77
  10.7 27.8 %copy-start.2 = (s32[8192]{0:T(1024)S(1)}, s32[8192]{0:T(1024)}, u32[]{:S(2)}) copy-start(s32[8192]{0:T(1024)} %param.14) | copy-start | bytes 98308
  10.7 27.8 %copy-start.1 = (s32[8192]{0:T(1024)S(1)}, s32[8192]{0:T(1024)}, u32[]{:S(2)}) copy-start(s32[8192]{0:T(1024)} %param.13) | copy-start | bytes 98308
  81.9 50.2 %reduce-scatter.5.cloned.1.call-start = ((), (), s32[]{:S(2)}) async-start(), calls=%async_computation.4 | async-start | bytes 327680 | tf_op jit(solution)/shard_map/reduce_scatter | solution.py:78
Sparse Core Ops, SparseCore 0:
  8.9 30.6 all-gather.1
  82.0 28.9 reduce-scatter.2
  113.5 18.5 reduce-scatter.4
where the time goes:
time: 168 us
  local copies, waits for them, and re-layouts  58.4 us (35%)
  waiting for transfers between devices  51.9 us (31%)
  matrix products  26.3 us (16%)
  blocking collectives  13.4 us (8%)
  between operations  13.2 us (8%)
  other arithmetic  4.68 us (3%)
    reduce_scatter x1, waiting for transfers between devices, local(): lax.psum_scatter(phi_part, 'rows', scatter_dimension=1, tiled=True)  29.1 us
    gather x1, local copies, waits for them, and re-layouts, one_block(): jnp.take(right_side, feat_col, axis=1)  27.7 us
    gather x1, local copies, waits for them, and re-layouts, one_block(): jnp.take(left_side, left_index, axis=1)  27.7 us
    reduce_scatter x1, waiting for transfers between devices, local(): lax.psum_scatter(by_feature, 'ex', scatter_dimension=0, tiled=True)  21.1 us
    dot_general x1, matrix products, local(): lax.dot_general(phi_all, inverse_rows, (((1,), (1,)), ((), ())), preferre...  15.1 us
    all_gather x1, blocking collectives, local(): phi_all = lax.all_gather(phi_low, 'rows', axis=1, tiled=True)  13.4 us
    dot_general x1, matrix products, one_block(): return total + jnp.dot(member, products, precision=exact_mode)  7.22 us
  transfers between devices with their start and end apart: 3, of which 3 were waited for; matrix products, arithmetic and copies ran while one was open for 19% of the time, Pallas kernels for 0%

commit v1 on v0

v1 whole, which is shorter than its diff:
```python
import functools
import math

import jax
import jax.numpy as jnp
from jax import lax
from jax.experimental import pallas as pl
from jax.experimental.pallas import tpu as pltpu
from jax.sharding import PartitionSpec as P


def signs(first_bits, second_bits):
    odd = lax.population_count(first_bits & second_bits) & 1
    return (1 - 2 * odd).astype(jnp.float32).astype(jnp.bfloat16)


def sign_rows(first, count, step, picks):
    inner = lax.broadcasted_iota(jnp.int32, (step, picks.shape[1]), 0)
    table = signs(inner, picks)
    parts = [table * signs(jnp.zeros_like(picks) + (first + n * step), picks) for n in range(count)]
    return parts[0] if count == 1 else jnp.concatenate(parts, axis=0)


def loop(count, body):
    if count <= 4:
        for n in range(count):
            body(n)
    else:
        lax.fori_loop(0, count, lambda n, c: (body(n), c)[1], 0)


def when(cond, body):
    if isinstance(cond, bool):
        if cond:
            body()
    else:
        pl.when(cond)(body)


def kernel(
    row_count,
    ex_count,
    norm_scale,
    hid_ref,
    cot_ref,
    len_ref,
    rsign_ref,
    csign_ref,
    frow_ref,
    fcol_ref,
    inv_ref,
    out_ref,
    hid_all,
    cot_signed,
    right_buf,
    part_buf,
    ex_in,
    row_in,
    low_all,
    inv_buf,
    total_buf,
    inv_sem,
    hid_send,
    hid_recv,
    ex_send,
    ex_recv,
    row_send,
    row_recv,
    low_send,
    low_recv,
):
    row = lax.axis_index("rows")
    ex = lax.axis_index("ex")
    tok_dev, width = hid_ref.shape
    cot_width = cot_ref.shape[1]
    features = frow_ref.shape[1]
    own = features // row_count
    examples = len_ref.shape[1]
    chunk = min(own, 512)
    ex_steps = ex_count.bit_length() - 1

    def inv_copy(n):
        q = lax.rem(row + n, row_count)
        cols = pl.ds(pl.multiple_of(q * own, 128), own)
        return pltpu.make_async_copy(inv_ref.at[:, cols], inv_buf.at[q], inv_sem.at[q])

    barrier = pltpu.get_barrier_semaphore()

    def greet(n):
        pl.semaphore_signal(
            barrier,
            inc=1,
            device_id={"rows": lax.rem(row + n + 1, row_count)},
            device_id_type=pl.DeviceIdType.MESH,
        )

    loop(row_count - 1, greet)

    def bit_of(step):
        return lax.rem(ex // (1 << step), 2)

    def partner_of(step):
        return ex + (1 - 2 * bit_of(step)) * (1 << step)

    for step in range(ex_steps):
        pl.semaphore_signal(
            barrier,
            inc=1,
            device_id={"ex": partner_of(step)},
            device_id_type=pl.DeviceIdType.MESH,
        )
    loop(row_count, lambda n: inv_copy(n).start())
    hid_all[row] = hid_ref[...] * rsign_ref[...].astype(jnp.float32).astype(jnp.bfloat16)
    if csign_ref.shape[1] == cot_width:
        col_sign = csign_ref[...]
    else:
        col_sign = csign_ref[:, pl.ds(pl.multiple_of(row * cot_width, 128), cot_width)]
    cot_signed[...] = cot_ref[...] * col_sign.astype(jnp.float32).astype(jnp.bfloat16)
    lens = jnp.broadcast_to(len_ref[...].astype(jnp.float32), (examples, examples))
    e_row = lax.broadcasted_iota(jnp.int32, (examples, examples), 0)
    e_col = lax.broadcasted_iota(jnp.int32, (examples, examples), 1)
    ends = jnp.sum(jnp.where(e_col <= e_row, lens, 0.0), axis=1, keepdims=True)
    starts = jnp.sum(jnp.where(e_col < e_row, lens, 0.0), axis=1, keepdims=True)
    spots = ex * tok_dev + lax.broadcasted_iota(jnp.int32, (examples, tok_dev), 1)
    spots = spots.astype(jnp.float32)
    member = jnp.where((spots >= starts) & (spots < ends), 1.0, 0.0).astype(jnp.bfloat16)
    pl.semaphore_wait(barrier, row_count - 1 + ex_steps)

    def hid_copy(n, incoming=False):
        to = lax.rem(row + n + 1, row_count)
        block = lax.rem(row - n - 1 + row_count, row_count) if incoming else row
        return pltpu.make_async_remote_copy(
            src_ref=hid_all.at[block],
            dst_ref=hid_all.at[block],
            send_sem=hid_send.at[n],
            recv_sem=hid_recv.at[n],
            device_id={"rows": to},
            device_id_type=pl.DeviceIdType.MESH,
        )

    loop(row_count - 1, lambda n: hid_copy(n).start())

    def block_of(i):
        return lax.rem(row + 1 + i, row_count)

    def picks_of(ref, i, c):
        at = pl.multiple_of(block_of(i) * own + c * chunk, 128)
        return ref[:, pl.ds(at, chunk)]

    inner = min(cot_width, 128)

    def right_side(i):
        def one(c):
            table = sign_rows(row * cot_width, cot_width // inner, inner, picks_of(fcol_ref, i, c))
            at = c * chunk if isinstance(c, int) else pl.multiple_of(c * chunk, 128)
            right_buf[i, :, pl.ds(at, chunk)] = jnp.dot(
                cot_signed[...], table, preferred_element_type=jnp.float32
            )

        loop(own // chunk, one)

    group = min(row_count, 4)

    def features_of(i):
        def one(c):
            picks = picks_of(frow_ref, i, c)

            def some(g, left):
                acts = jnp.concatenate([hid_all[g * group + n] for n in range(group)], axis=1)
                table = sign_rows(g * group * width, group, width, picks)
                return left + jnp.dot(acts, table, preferred_element_type=jnp.float32)

            left = jnp.zeros((tok_dev, chunk), jnp.float32)
            if row_count == group:
                left = some(0, left)
            else:
                left = lax.fori_loop(0, row_count // group, some, left)
            at = c * chunk if isinstance(c, int) else pl.multiple_of(c * chunk, 128)
            products = left * right_buf[i, :, pl.ds(at, chunk)]
            high = products.astype(jnp.bfloat16)
            rest = (products - high.astype(jnp.float32)).astype(jnp.bfloat16)
            sums = jnp.dot(member, high, preferred_element_type=jnp.float32)
            sums = sums + jnp.dot(member, rest, preferred_element_type=jnp.float32)
            part_buf[i, :, :, pl.ds(at, chunk)] = sums.reshape(ex_count, examples // ex_count, chunk)

        loop(own // chunk, one)

    def ex_copies(i, step):
        size = 1 << step
        first = ex_count - (ex_count >> step)
        copies = []
        for m in range(ex_count >> (step + 1)):
            away = lax.rem(ex, size) + (1 - bit_of(step)) * size + m * 2 * size
            slot = first + m
            copies.append(
                pltpu.make_async_remote_copy(
                    src_ref=part_buf.at[i, away],
                    dst_ref=ex_in.at[i, slot],
                    send_sem=ex_send.at[i, slot],
                    recv_sem=ex_recv.at[i, slot],
                    device_id={"ex": partner_of(step)},
                    device_id_type=pl.DeviceIdType.MESH,
                )
            )
        return copies

    def ex_start(i, step):
        for copy in ex_copies(i, step):
            copy.start()

    def ex_finish(i, step):
        size = 1 << step
        first = ex_count - (ex_count >> step)
        for m, copy in enumerate(ex_copies(i, step)):
            copy.wait_recv()
            mine = lax.rem(ex, 2 * size) + m * 2 * size
            part_buf[i, mine] = part_buf[i, mine] + ex_in[i, first + m]

    def row_copy(i):
        return pltpu.make_async_remote_copy(
            src_ref=part_buf.at[i, ex],
            dst_ref=row_in.at[i],
            send_sem=row_send.at[i],
            recv_sem=row_recv.at[i],
            device_id={"rows": block_of(i)},
            device_id_type=pl.DeviceIdType.MESH,
        )

    def stage(i, step):
        def work():
            if step > 0:
                ex_finish(i, step - 1)
            if step < ex_steps:
                ex_start(i, step)
            else:
                when(i < row_count - 1, lambda: row_copy(i).start())

        return work

    right_side(0)
    if row_count > 1:
        right_side(1)
    loop(row_count - 1, lambda n: hid_copy(n, True).wait_recv())

    def block_step(i):
        features_of(i)
        stage(i, 0)()
        for step in range(1, ex_steps + 1):
            when(i >= step, stage(i - step, step))
        when(i + 2 < row_count, lambda: right_side(i + 2))

    loop(row_count, block_step)
    for late in range(1, ex_steps + 1):
        for step in range(late, ex_steps + 1):
            if row_count - 1 + late - step >= 0:
                stage(row_count - 1 + late - step, step)()

    total_buf[...] = part_buf[row_count - 1, ex]

    def add_row(n):
        row_copy(n).wait_recv()
        total_buf[...] = total_buf[...] + row_in[n]

    loop(row_count - 1, add_row)
    low_all[row] = (total_buf[...] * norm_scale).astype(jnp.bfloat16)

    def low_copy(n, incoming=False):
        block = lax.rem(row - n - 1 + row_count, row_count) if incoming else row
        return pltpu.make_async_remote_copy(
            src_ref=low_all.at[block],
            dst_ref=low_all.at[block],
            send_sem=low_send.at[n],
            recv_sem=low_recv.at[n],
            device_id={"rows": lax.rem(row + n + 1, row_count)},
            device_id_type=pl.DeviceIdType.MESH,
        )

    loop(row_count - 1, lambda n: low_copy(n).start())
    tile = min(own, 256)

    def score_block(n):
        q = lax.rem(row - n + row_count, row_count)
        when(n > 0, lambda: low_copy(n - 1, True).wait_recv())
        pltpu.make_async_copy(
            inv_ref.at[:, pl.ds(pl.multiple_of(q * own, 128), own)], inv_buf.at[q], inv_sem.at[q]
        ).wait()
        low = low_all[q]

        def one(j, carry):
            at = pl.multiple_of(j * tile, 128)
            got = lax.dot_general(
                low,
                inv_buf[q, pl.ds(at, tile), :],
                (((1,), (1,)), ((), ())),
                preferred_element_type=jnp.float32,
            )
            before = jnp.where(n > 0, total_buf[:, pl.ds(at, tile)], 0.0)
            total_buf[:, pl.ds(at, tile)] = before + got
            return carry

        lax.fori_loop(0, own // tile, one, 0)

    loop(row_count, score_block)
    out_ref[...] = total_buf[...].astype(out_ref.dtype)
    loop(row_count - 1, lambda n: hid_copy(n).wait_send())
    loop(row_count - 1, lambda n: low_copy(n).wait_send())
    loop(row_count - 1, lambda n: row_copy(n).wait_send())

    def ex_sent(i):
        for step in range(ex_steps):
            for copy in ex_copies(i, step):
                copy.wait_send()

    loop(row_count, ex_sent)


def local(hidden_acts, cotangent, lengths, row_signs, col_signs, feat_row, feat_col, inverse_rows):
    row_count = lax.axis_size("rows")
    ex_count = lax.axis_size("ex")
    tok_dev, width = hidden_acts.shape
    cot_width = cotangent.shape[1]
    features = feat_row.shape[0]
    examples = lengths.shape[0]
    own = features // row_count
    owned = examples // ex_count
    norm_scale = 1.0 / math.sqrt(width * row_count * col_signs.shape[0])
    if cot_width % 128 != 0:
        col_signs = lax.dynamic_slice(col_signs, (lax.axis_index("rows") * cot_width,), (cot_width,))
    vmem = pl.BlockSpec(memory_space=pltpu.VMEM)
    others = max(row_count - 1, 1)
    dma = pltpu.SemaphoreType.DMA
    return pl.pallas_call(
        functools.partial(kernel, row_count, ex_count, norm_scale),
        out_shape=jax.ShapeDtypeStruct((owned, own), jnp.bfloat16),
        in_specs=[vmem] * 7 + [pl.BlockSpec(memory_space=pl.ANY)],
        out_specs=vmem,
        scratch_shapes=[
            pltpu.VMEM((row_count, tok_dev, width), jnp.bfloat16),
            pltpu.VMEM((tok_dev, cot_width), jnp.bfloat16),
            pltpu.VMEM((row_count, tok_dev, own), jnp.float32),
            pltpu.VMEM((row_count, ex_count, owned, own), jnp.float32),
            pltpu.VMEM((row_count, max(ex_count - 1, 1), owned, own), jnp.float32),
            pltpu.VMEM((others, owned, own), jnp.float32),
            pltpu.VMEM((row_count, owned, own), jnp.bfloat16),
            pltpu.VMEM((row_count, own, own), jnp.bfloat16),
            pltpu.VMEM((owned, own), jnp.float32),
            dma((row_count,)),
            dma((others,)),
            dma((others,)),
            dma((row_count, max(ex_count - 1, 1))),
            dma((row_count, max(ex_count - 1, 1))),
            dma((others,)),
            dma((others,)),
            dma((others,)),
            dma((others,)),
        ],
        compiler_params=pltpu.CompilerParams(
            collective_id=0, has_side_effects=True, vmem_limit_bytes=60 * 1024 * 1024
        ),
        name="features_and_scores",
    )(
        hidden_acts,
        cotangent,
        lengths.reshape(1, -1),
        row_signs.reshape(1, -1),
        col_signs.reshape(1, -1),
        feat_row.reshape(1, -1),
        feat_col.reshape(1, -1),
        inverse_rows,
    )


def solution(mesh):
    placed = (
        P(("parts", "ex"), "rows"),
        P(("parts", "ex"), "rows"),
        P("parts"),
        P("rows"),
        P(),
        P(),
        P(),
        P("rows", None),
    )
    return jax.shard_map(
        local, mesh=mesh, in_specs=placed, out_specs=P(("parts", "ex"), "rows"), check_vma=False
    )
```

time: 168 us -> 40.8 us (0.24)
  local copies, waits for them, and re-layouts: 58.4 us -> 1.38 us
  waiting for transfers between devices: 51.9 us -> 0 us
  Pallas kernels: 0 us -> 39.2 us
  matrix products: 26.3 us -> 0 us
  blocking collectives: 13.4 us -> 0 us
  between operations: 13.2 us -> 0.01 us
  other arithmetic: 4.68 us -> 0 us
    gather x2 -> x0, local copies, waits for them, and re-layouts: 55.4 us -> none  [the longest x1 27.7 us: one_block(): jnp.take(right_side, feat_col, axis=1)]
    reduce_scatter x2 -> x0, waiting for transfers between devices: 50.2 us -> none  [the longest x1 29.1 us: local(): lax.psum_scatter(phi_part, 'rows', scatter_dimension=1, tiled=True)]
    pallas_call x0 -> x1, Pallas kernels: none -> 39.2 us  [local(): pl.pallas_call(functools.partial(kernel, row_count, ex_count, norm_scale)...]
    dot_general x5 -> x0, matrix products: 26.3 us -> none  [the longest x1 15.1 us: local(): lax.dot_general(phi_all, inverse_rows, (((1,), (1,)), ((), ())), preferre...]
    all_gather x1 -> x0, blocking collectives: 13.4 us -> none  [local(): phi_all = lax.all_gather(phi_low, 'rows', axis=1, tiled=True)]
    convert_element_type x3 -> x0, other arithmetic: 2.22 us -> none  [the longest x1 0.84 us: local(): phi_low = phi_own.astype(jnp.bfloat16)]
    reshape x1 -> x0, local copies, waits for them, and re-layouts: 2.01 us -> none  [kron_signed(): return shaped.reshape(tokens, outer_size * inner_size)]
  transfers between devices with their start and end apart: 3 -> 0, of which waited for: 3 -> 0; matrix products, arithmetic and copies ran while one was open for 19% -> 0% of each run, Pallas kernels for 0% -> 0%
where the time goes in v1:
time: 40.8 us; the launch traced here: 40.6 us
  Pallas kernels  39.2 us (96%)
  local copies, waits for them, and re-layouts  1.38 us (3%)
    pallas_call x1, Pallas kernels, local(): pl.pallas_call(functools.partial(kernel, row_count, ex_count, norm_scale)...  39.2 us
    unnamed x1, local copies, waits for them, and re-layouts  1.38 us

profile of v1, /device:TPU:0, one launch (start us, length us, event | category | flops | bytes accessed | tf_op | source)
XLA Modules:
  0.0 40.6 jit_solution(7531052507173798554)
XLA Ops:
  0.0 39.2 %features_and_scores.1 = bf16[8,2048]{1,0:T(8,128)(2,1)} custom-call(bf16[128,128]{1,0:T(8,128)(2,1)} %hid_ref.1, bf16[128,1024]{1,0:T(8,128)(2,1)} %cot_ref.1, s32[1,32]{1,0:T(1,128)} %bitcast.8, s32[1,128]{1,0:T(1,128)} %bitcast.9, s32[1,4096]{1,0:T(1,128)} %bitcast.7, s32[1,8192]{1,0:T(1,128)} %bitcast.5, s32[1,8192]{1,0:T(1,128)} %bitcast.6, ...), custom_call_target="tpu_custom_call" | custom-call | tf_op jit(solution)/shard_map/features_and_scores/pallas_call | solution.py:332
  39.2 1.4 %copy.10 = bf16[8,2048]{1,0:T(8,128)(2,1)} copy(bf16[8,2048]{1,0:T(8,128)(2,1)} %features_and_scores.1) | data formatting | bytes 65536

commit v2 on v1

--- a/solution.py
+++ b/solution.py
@@ -56,7 +56,8 @@
     part_buf,
     ex_in,
     row_in,
-    low_all,
+    score_out,
+    score_in,
     inv_buf,
     total_buf,
     inv_sem,
@@ -66,8 +67,8 @@
     ex_recv,
     row_send,
     row_recv,
-    low_send,
-    low_recv,
+    score_send,
+    score_recv,
 ):
     row = lax.axis_index("rows")
     ex = lax.axis_index("ex")
@@ -79,10 +80,12 @@
     chunk = min(own, 512)
     ex_steps = ex_count.bit_length() - 1
 
+    def block_of(i):
+        return lax.rem(row + 1 + i, row_count)
+
     def inv_copy(n):
-        q = lax.rem(row + n, row_count)
-        cols = pl.ds(pl.multiple_of(q * own, 128), own)
-        return pltpu.make_async_copy(inv_ref.at[:, cols], inv_buf.at[q], inv_sem.at[q])
+        cols = pl.ds(pl.multiple_of(block_of(n) * own, 128), own)
+        return pltpu.make_async_copy(inv_ref.at[:, cols], inv_buf.at[n], inv_sem.at[n])
 
     barrier = pltpu.get_barrier_semaphore()
 
@@ -139,9 +142,6 @@
         )
 
     loop(row_count - 1, lambda n: hid_copy(n).start())
-
-    def block_of(i):
-        return lax.rem(row + 1 + i, row_count)
 
     def picks_of(ref, i, c):
         at = pl.multiple_of(block_of(i) * own + c * chunk, 128)
@@ -237,9 +237,7 @@
 
         return work
 
-    right_side(0)
-    if row_count > 1:
-        right_side(1)
+    loop(row_count, right_side)
     loop(row_count - 1, lambda n: hid_copy(n, True).wait_recv())
 
     def block_step(i):
@@ -247,7 +245,6 @@
         stage(i, 0)()
         for step in range(1, ex_steps + 1):
             when(i >= step, stage(i - step, step))
-        when(i + 2 < row_count, lambda: right_side(i + 2))
 
     loop(row_count, block_step)
     for late in range(1, ex_steps + 1):
@@ -262,48 +259,43 @@
         total_buf[...] = total_buf[...] + row_in[n]
 
     loop(row_count - 1, add_row)
-    low_all[row] = (total_buf[...] * norm_scale).astype(jnp.bfloat16)
-
-    def low_copy(n, incoming=False):
-        block = lax.rem(row - n - 1 + row_count, row_count) if incoming else row
+    low = (total_buf[...] * norm_scale).astype(jnp.bfloat16)
+
+    def score_copy(n):
         return pltpu.make_async_remote_copy(
-            src_ref=low_all.at[block],
-            dst_ref=low_all.at[block],
-            send_sem=low_send.at[n],
-            recv_sem=low_recv.at[n],
-            device_id={"rows": lax.rem(row + n + 1, row_count)},
-            device_id_type=pl.DeviceIdType.MESH,
-        )
-
-    loop(row_count - 1, lambda n: low_copy(n).start())
-    tile = min(own, 256)
+            src_ref=score_out.at[n],
+            dst_ref=score_in.at[n],
+            send_sem=score_send.at[n],
+            recv_sem=score_recv.at[n],
+            device_id={"rows": block_of(n)},
+            device_id_type=pl.DeviceIdType.MESH,
+        )
+
+    tile = min(own, 512)
 
     def score_block(n):
-        q = lax.rem(row - n + row_count, row_count)
-        when(n > 0, lambda: low_copy(n - 1, True).wait_recv())
-        pltpu.make_async_copy(
-            inv_ref.at[:, pl.ds(pl.multiple_of(q * own, 128), own)], inv_buf.at[q], inv_sem.at[q]
-        ).wait()
-        low = low_all[q]
-
-        def one(j, carry):
-            at = pl.multiple_of(j * tile, 128)
-            got = lax.dot_general(
-                low,
-                inv_buf[q, pl.ds(at, tile), :],
-                (((1,), (1,)), ((), ())),
-                preferred_element_type=jnp.float32,
+        inv_copy(n).wait()
+
+        def one(j):
+            at = j * tile if isinstance(j, int) else pl.multiple_of(j * tile, 128)
+            score_out[n, :, pl.ds(at, tile)] = jnp.dot(
+                low, inv_buf[n, :, pl.ds(at, tile)], preferred_element_type=jnp.float32
             )
-            before = jnp.where(n > 0, total_buf[:, pl.ds(at, tile)], 0.0)
-            total_buf[:, pl.ds(at, tile)] = before + got
-            return carry
-
-        lax.fori_loop(0, own // tile, one, 0)
+
+        loop(own // tile, one)
+        when(n < row_count - 1, lambda: score_copy(n).start())
 
     loop(row_count, score_block)
+    total_buf[...] = score_out[row_count - 1]
+
+    def add_score(n):
+        score_copy(n).wait_recv()
+        total_buf[...] = total_buf[...] + score_in[n]
+
+    loop(row_count - 1, add_score)
     out_ref[...] = total_buf[...].astype(out_ref.dtype)
     loop(row_count - 1, lambda n: hid_copy(n).wait_send())
-    loop(row_count - 1, lambda n: low_copy(n).wait_send())
+    loop(row_count - 1, lambda n: score_copy(n).wait_send())
     loop(row_count - 1, lambda n: row_copy(n).wait_send())
 
     def ex_sent(i):
@@ -341,7 +333,8 @@
             pltpu.VMEM((row_count, ex_count, owned, own), jnp.float32),
             pltpu.VMEM((row_count, max(ex_count - 1, 1), owned, own), jnp.float32),
             pltpu.VMEM((others, owned, own), jnp.float32),
-            pltpu.VMEM((row_count, owned, own), jnp.bfloat16),
+            pltpu.VMEM((row_count, owned, own), jnp.float32),
+            pltpu.VMEM((others, owned, own), jnp.float32),
             pltpu.VMEM((row_count, own, own), jnp.bfloat16),
             pltpu.VMEM((owned, own), jnp.float32),
             dma((row_count,)),

time: 40.8 us -> 34.5 us (0.85)
  Pallas kernels: 39.2 us -> 33 us
    pallas_call x1, Pallas kernels: 39.2 us -> 33 us  [local(): pl.pallas_call(functools.partial(kernel, row_count, ex_count, norm_scale)...]
where the time goes in v2:
time: 34.5 us; the launch traced here: 34.3 us
  Pallas kernels  33 us (96%)
  local copies, waits for them, and re-layouts  1.38 us (4%)
    pallas_call x1, Pallas kernels, local(): pl.pallas_call(functools.partial(kernel, row_count, ex_count, norm_scale)...  33 us
    unnamed x1, local copies, waits for them, and re-layouts  1.38 us

profile of v2, /device:TPU:0, one launch (start us, length us, event | category | flops | bytes accessed | tf_op | source)
XLA Modules:
  0.0 34.3 jit_solution(2128938647370749359)
XLA Ops:
  0.0 33.0 %features_and_scores.1 = bf16[8,2048]{1,0:T(8,128)(2,1)} custom-call(bf16[128,128]{1,0:T(8,128)(2,1)} %hid_ref.1, bf16[128,1024]{1,0:T(8,128)(2,1)} %cot_ref.1, s32[1,32]{1,0:T(1,128)} %bitcast.8, s32[1,128]{1,0:T(1,128)} %bitcast.9, s32[1,4096]{1,0:T(1,128)} %bitcast.7, s32[1,8192]{1,0:T(1,128)} %bitcast.5, s32[1,8192]{1,0:T(1,128)} %bitcast.6, ...), custom_call_target="tpu_custom_call" | custom-call | tf_op jit(solution)/shard_map/features_and_scores/pallas_call | solution.py:324
  33.0 1.4 %copy.10 = bf16[8,2048]{1,0:T(8,128)(2,1)} copy(bf16[8,2048]{1,0:T(8,128)(2,1)} %features_and_scores.1) | data formatting | bytes 65536

commit v3 on v2

--- a/solution.py
+++ b/solution.py
@@ -55,6 +55,7 @@
     right_buf,
     part_buf,
     ex_in,
+    row_out,
     row_in,
     score_out,
     score_in,
@@ -218,7 +219,7 @@
 
     def row_copy(i):
         return pltpu.make_async_remote_copy(
-            src_ref=part_buf.at[i, ex],
+            src_ref=row_out.at[i],
             dst_ref=row_in.at[i],
             send_sem=row_send.at[i],
             recv_sem=row_recv.at[i],
@@ -233,7 +234,13 @@
             if step < ex_steps:
                 ex_start(i, step)
             else:
-                when(i < row_count - 1, lambda: row_copy(i).start())
+
+
+                def send():
+                    row_out[i] = part_buf[i, ex].astype(row_out.dtype)
+                    row_copy(i).start()
+
+                when(i < row_count - 1, send)
 
         return work
 
@@ -256,7 +263,7 @@
 
     def add_row(n):
         row_copy(n).wait_recv()
-        total_buf[...] = total_buf[...] + row_in[n]
+        total_buf[...] = total_buf[...] + row_in[n].astype(jnp.float32)
 
     loop(row_count - 1, add_row)
     low = (total_buf[...] * norm_scale).astype(jnp.bfloat16)
@@ -278,19 +285,24 @@
 
         def one(j):
             at = j * tile if isinstance(j, int) else pl.multiple_of(j * tile, 128)
-            score_out[n, :, pl.ds(at, tile)] = jnp.dot(
-                low, inv_buf[n, :, pl.ds(at, tile)], preferred_element_type=jnp.float32
-            )
+            got = jnp.dot(low, inv_buf[n, :, pl.ds(at, tile)], preferred_element_type=jnp.float32)
+
+            def keep():
+                total_buf[:, pl.ds(at, tile)] = got
+
+            def give():
+                score_out[n, :, pl.ds(at, tile)] = got.astype(score_out.dtype)
+
+            when(n == row_count - 1, keep)
+            when(n < row_count - 1, give)
 
         loop(own // tile, one)
         when(n < row_count - 1, lambda: score_copy(n).start())
 
     loop(row_count, score_block)
-    total_buf[...] = score_out[row_count - 1]
-
     def add_score(n):
         score_copy(n).wait_recv()
-        total_buf[...] = total_buf[...] + score_in[n]
+        total_buf[...] = total_buf[...] + score_in[n].astype(jnp.float32)
 
     loop(row_count - 1, add_score)
     out_ref[...] = total_buf[...].astype(out_ref.dtype)
@@ -332,9 +344,10 @@
             pltpu.VMEM((row_count, tok_dev, own), jnp.float32),
             pltpu.VMEM((row_count, ex_count, owned, own), jnp.float32),
             pltpu.VMEM((row_count, max(ex_count - 1, 1), owned, own), jnp.float32),
-            pltpu.VMEM((others, owned, own), jnp.float32),
-            pltpu.VMEM((row_count, owned, own), jnp.float32),
-            pltpu.VMEM((others, owned, own), jnp.float32),
+            pltpu.VMEM((others, owned, own), jnp.bfloat16),
+            pltpu.VMEM((others, owned, own), jnp.bfloat16),
+            pltpu.VMEM((others, owned, own), jnp.bfloat16),
+            pltpu.VMEM((others, owned, own), jnp.bfloat16),
             pltpu.VMEM((row_count, own, own), jnp.bfloat16),
             pltpu.VMEM((owned, own), jnp.float32),
             dma((row_count,)),

time: 34.5 us -> 33 us (0.957)
  Pallas kernels: 33 us -> 31.5 us
    pallas_call x1, Pallas kernels: 33 us -> 31.5 us  [local(): pl.pallas_call(functools.partial(kernel, row_count, ex_count, norm_scale)...]
where the time goes in v3:
time: 33 us; the launch traced here: 32.8 us
  Pallas kernels  31.5 us (95%)
  local copies, waits for them, and re-layouts  1.38 us (4%)
    pallas_call x1, Pallas kernels, local(): pl.pallas_call(functools.partial(kernel, row_count, ex_count, norm_scale)...  31.5 us
    unnamed x1, local copies, waits for them, and re-layouts  1.38 us

profile of v3, /device:TPU:0, one launch (start us, length us, event | category | flops | bytes accessed | tf_op | source)
XLA Modules:
  0.0 32.8 jit_solution(11966895490087016586)
XLA Ops:
  0.0 31.5 %features_and_scores.1 = bf16[8,2048]{1,0:T(8,128)(2,1)} custom-call(bf16[128,128]{1,0:T(8,128)(2,1)} %hid_ref.1, bf16[128,1024]{1,0:T(8,128)(2,1)} %cot_ref.1, s32[1,32]{1,0:T(1,128)} %bitcast.8, s32[1,128]{1,0:T(1,128)} %bitcast.9, s32[1,4096]{1,0:T(1,128)} %bitcast.7, s32[1,8192]{1,0:T(1,128)} %bitcast.5, s32[1,8192]{1,0:T(1,128)} %bitcast.6, ...), custom_call_target="tpu_custom_call" | custom-call | tf_op jit(solution)/shard_map/features_and_scores/pallas_call | solution.py:336
  31.5 1.4 %copy.10 = bf16[8,2048]{1,0:T(8,128)(2,1)} copy(bf16[8,2048]{1,0:T(8,128)(2,1)} %features_and_scores.1) | data formatting | bytes 65536

commit v4 on v3

--- a/solution.py
+++ b/solution.py
@@ -248,10 +248,10 @@
     loop(row_count - 1, lambda n: hid_copy(n, True).wait_recv())
 
     def block_step(i):
+        for step in range(ex_steps, 0, -1):
+            when(i >= step, stage(i - step, step))
         features_of(i)
         stage(i, 0)()
-        for step in range(1, ex_steps + 1):
-            when(i >= step, stage(i - step, step))
 
     loop(row_count, block_step)
     for late in range(1, ex_steps + 1):

time: 33 us -> 34.6 us (1.048)
  Pallas kernels: 31.5 us -> 33.1 us
    pallas_call x1, Pallas kernels: 31.5 us -> 33.1 us  [local(): pl.pallas_call(functools.partial(kernel, row_count, ex_count, norm_scale)...]
where the time goes in v4:
time: 34.6 us; the launch traced here: 34.4 us
  Pallas kernels  33.1 us (96%)
  local copies, waits for them, and re-layouts  1.38 us (4%)
    pallas_call x1, Pallas kernels, local(): pl.pallas_call(functools.partial(kernel, row_count, ex_count, norm_scale)...  33.1 us
    unnamed x1, local copies, waits for them, and re-layouts  1.38 us

profile of v4, /device:TPU:0, one launch (start us, length us, event | category | flops | bytes accessed | tf_op | source)
XLA Modules:
  0.0 34.4 jit_solution(15560116009864578618)
XLA Ops:
  0.0 33.1 %features_and_scores.1 = bf16[8,2048]{1,0:T(8,128)(2,1)} custom-call(bf16[128,128]{1,0:T(8,128)(2,1)} %hid_ref.1, bf16[128,1024]{1,0:T(8,128)(2,1)} %cot_ref.1, s32[1,32]{1,0:T(1,128)} %bitcast.8, s32[1,128]{1,0:T(1,128)} %bitcast.9, s32[1,4096]{1,0:T(1,128)} %bitcast.7, s32[1,8192]{1,0:T(1,128)} %bitcast.5, s32[1,8192]{1,0:T(1,128)} %bitcast.6, ...), custom_call_target="tpu_custom_call" | custom-call | tf_op jit(solution)/shard_map/features_and_scores/pallas_call | solution.py:336
  33.1 1.4 %copy.10 = bf16[8,2048]{1,0:T(8,128)(2,1)} copy(bf16[8,2048]{1,0:T(8,128)(2,1)} %features_and_scores.1) | data formatting | bytes 65536
